TPU v7x, 128 devices: a whole 4x4x4 slice. The times are simulated.
128 devices in a mesh: dp: 64 (over z, y, x), tensor: 2 (over core).
Axes of the slice: x: 4, y: 4, z: 4, core: 2. Of those that a mesh axis runs over, the one named last changes fastest.
Arguments:
- square_grad: float32 [32, 2359296], P(None, ('dp', 'tensor')), may hold values from -80 to 80
- square_state: float32 [32, 2359296], P(None, ('dp', 'tensor')), may hold values from -6 to 6
- swiglu_grad: float32 [24, 6291456], P(None, ('dp', 'tensor')), may hold values from -80 to 80
- swiglu_state: float32 [24, 6291456], P(None, ('dp', 'tensor')), may hold values from -6 to 6
- square_order: int32 [32], replicated, may hold values from 0 to 31, each once
- swiglu_order: int32 [24], replicated, may hold values from 0 to 23, each once
- owners: int32 [56], replicated, may hold values from 0 to 63, as said below
- vector_values: float32 [172032], P(('dp', 'tensor')), may hold values from -6 to 6
- vector_grad: float32 [172032], P(('dp', 'tensor')), may hold values from -6 to 6
- vector_first: float32 [172032], P(('dp', 'tensor')), may hold values from -4 to 4
- vector_second: float32 [172032], P(('dp', 'tensor')), may hold values from 0.01 to 1
- embed_values: float32 [8192, 1536], P('dp', 'tensor'), may hold values from -6 to 6
- embed_grad: float32 [8192, 1536], P('dp', 'tensor'), may hold values from -6 to 6
- embed_first: float32 [8192, 1536], P('dp', 'tensor'), may hold values from -4 to 4
- embed_second: float32 [8192, 1536], P('dp', 'tensor'), may hold values from 0.01 to 1
- embed_ranges: int32 [16, 2], replicated, may hold values from 0 to 8192, as said below
Outputs:
- square_next: float32 [32, 2359296], P(None, ('dp', 'tensor'))
- swiglu_next: float32 [24, 6291456], P(None, ('dp', 'tensor'))
- square_update: bfloat16 [32, 1536, 1536], P(None, 'dp', 'tensor')
- swiglu_update: bfloat16 [24, 1536, 4096], P(None, 'dp', 'tensor')
- owner_norms: float32 [64], P('dp')
- vector_step: float32 [172032], P(('dp', 'tensor'))
- first_vector: float32 [172032], P(('dp', 'tensor'))
- second_vector: float32 [172032], P(('dp', 'tensor'))
- embed_step: float32 [8192, 1536], P('dp', 'tensor')
- first_embed: float32 [8192, 1536], P('dp', 'tensor')
- second_embed: float32 [8192, 1536], P('dp', 'tensor')
Inputs may be any that keep to these rules, and one draw needn't show every extreme that they name: Different matrices have different owners. `square_order`: each matrix once. `swiglu_order`: each matrix once. `embed_ranges`: start < end in every row.
All inputs are finite; a program needn't handle non-finite values.
Results may differ from a plain program's by a relative error of at most 0.0065.
Values may be sent and summed in bfloat16 or wider, within the bound.
A program may use at most 128 MiB of HBM per device.

v0:
```python
import math
import jax
import jax.numpy as jnp
from jax import lax
from jax.sharding import PartitionSpec as P

D = 1536
FF = 4096
NS_STEPS = 2
QUINTIC_LINEAR = 3.4445
QUINTIC_CUBIC = -4.775
QUINTIC_FIFTH = 2.0315
MOMENTUM = 0.95
BIAS_FIRST = 1.0 - 0.9**10
BIAS_SECOND = 1.0 - 0.95**10


def momentum_terms(gradient, state):
    state_next = MOMENTUM * state + gradient
    return (state_next, (gradient + MOMENTUM * state_next).astype(jnp.bfloat16))


def adamw_terms(values, gradient, first, second):
    first_next = 0.9 * first + 0.1 * gradient
    second_next = 0.95 * second + 0.05 * gradient * gradient
    direction = (
        first_next / BIAS_FIRST / (jnp.sqrt(second_next / BIAS_SECOND) + 1e-08) + 0.1 * values
    )
    return (direction, first_next, second_next)


def table_lookup(table, positions):
    matches = positions[:, None] == jnp.arange(table.shape[0], dtype=jnp.int32)[None, :]
    return jnp.sum(jnp.where(matches, table[None, :], 0), axis=1)


def select_pieces(pieces, piece_owner, targets):
    matched = piece_owner[None, :] == targets[:, None]
    chosen = jnp.sum(
        jnp.where(matched, jnp.arange(piece_owner.shape[0], dtype=jnp.int32)[None, :], 0), axis=1
    )
    present = jnp.any(matched, axis=1)
    picked = jnp.where(present[:, None, None, None], pieces[chosen], jnp.zeros((), jnp.bfloat16))
    return (picked, chosen, present)


def local(
    square_grad,
    square_state,
    swiglu_grad,
    swiglu_state,
    square_order,
    swiglu_order,
    owners,
    vector_values,
    vector_grad,
    vector_first,
    vector_second,
    embed_values,
    embed_grad,
    embed_first,
    embed_second,
    embed_ranges,
):
    wide_count = lax.axis_size("dp")
    split_count = lax.axis_size("tensor")
    wide_index = lax.axis_index("dp")
    square_count = square_grad.shape[0]
    swiglu_count = swiglu_grad.shape[0]
    flat_rows = D // (wide_count * split_count)
    slot_width = FF // split_count
    square_width = D // split_count
    square_next, square_send = momentum_terms(square_grad, square_state)
    swiglu_next, swiglu_send = momentum_terms(swiglu_grad, swiglu_state)
    square_pieces = square_send.reshape(
        square_count, flat_rows, split_count, square_width
    ).transpose(0, 2, 1, 3)
    swiglu_pieces = swiglu_send.reshape(swiglu_count, flat_rows, split_count, slot_width).transpose(
        0, 2, 1, 3
    )
    square_owner = table_lookup(owners[:square_count], square_order)
    swiglu_owner = table_lookup(owners[square_count:], swiglu_order)
    targets = jnp.arange(wide_count, dtype=jnp.int32)
    square_mine = jnp.any(square_owner == wide_index)
    owned = square_mine | jnp.any(swiglu_owner == wide_index)
    factor = jnp.where(square_mine, jnp.float32(math.sqrt(D)), jnp.float32(math.sqrt(FF)))
    widened = jnp.pad(square_pieces, ((0, 0), (0, 0), (0, 0), (0, slot_width - square_width)))
    all_pieces = jnp.concatenate([widened, swiglu_pieces], axis=0)
    slot_owner = jnp.concatenate([square_owner, swiglu_owner])
    outgoing, chosen, present = select_pieces(all_pieces, slot_owner, targets)
    arrived = lax.all_to_all(
        outgoing.reshape(D, slot_width), ("dp", "tensor"), split_axis=0, concat_axis=0, tiled=True
    )
    iterate = arrived
    first_scale = jnp.float32(1.0)
    for round_index in range(NS_STEPS):
        current = iterate
        gram_part = lax.psum_scatter(
            jnp.einsum("rc,sc->rs", current, current, preferred_element_type=jnp.float32),
            "tensor",
            scatter_dimension=0,
            tiled=True,
        )
        if round_index == 0:
            squares_total = lax.psum(jnp.sum(gram_part * gram_part), "tensor")
            gram_scale = jnp.sqrt(squares_total) + 1e-06
            first_scale = gram_scale
        else:
            gram_scale = jnp.float32(1.0)
        normed_part = (gram_part / gram_scale).astype(jnp.bfloat16)
        squared = jnp.dot(
            normed_part,
            lax.all_gather(normed_part, "tensor", axis=0, tiled=True),
            preferred_element_type=jnp.float32,
        )
        polynomial = (
            QUINTIC_CUBIC * normed_part.astype(jnp.float32) + QUINTIC_FIFTH * squared
        ).astype(jnp.bfloat16)
        product = jnp.dot(
            lax.all_gather(polynomial, "tensor", axis=0, tiled=True),
            current,
            preferred_element_type=jnp.float32,
        )
        mixed = (QUINTIC_LINEAR * current.astype(jnp.float32) + product) / jnp.sqrt(gram_scale)
        if round_index == NS_STEPS - 1:
            iterate = (factor * mixed).astype(jnp.bfloat16)
        else:
            iterate = mixed.astype(jnp.bfloat16)
    returned = lax.all_to_all(
        iterate.reshape(wide_count, D // wide_count, slot_width),
        "dp",
        split_axis=0,
        concat_axis=0,
        tiled=True,
    )
    square_update = returned[owners[:square_count]][:, :, :square_width]
    swiglu_update = returned[owners[square_count:]]
    owner_norms = jnp.where(owned, 0.5 * jnp.log(first_scale), 0.0).reshape(1)
    vector_step, first_vector, second_vector = adamw_terms(
        vector_values, vector_grad, vector_first, vector_second
    )
    embed_rows = embed_values.shape[0]
    row_numbers = wide_index * embed_rows + jnp.arange(embed_rows, dtype=jnp.int32)
    inside = (row_numbers[:, None] >= embed_ranges[None, :, 0]) & (
        row_numbers[:, None] < embed_ranges[None, :, 1]
    )
    row_live = jnp.sum(inside.astype(jnp.int32), axis=1) > 0
    direction, first_next, second_next = adamw_terms(
        embed_values, embed_grad, embed_first, embed_second
    )
    embed_step = jnp.where(row_live[:, None], direction, 0.0)
    first_embed = jnp.where(row_live[:, None], first_next, embed_first)
    second_embed = jnp.where(row_live[:, None], second_next, embed_second)
    return (
        square_next,
        swiglu_next,
        square_update,
        swiglu_update,
        owner_norms,
        vector_step,
        first_vector,
        second_vector,
        embed_step,
        first_embed,
        second_embed,
    )


def solution(mesh):
    placed = (
        P(None, ("dp", "tensor")),
        P(None, ("dp", "tensor")),
        P(None, ("dp", "tensor")),
        P(None, ("dp", "tensor")),
        P(),
        P(),
        P(),
        P(("dp", "tensor")),
        P(("dp", "tensor")),
        P(("dp", "tensor")),
        P(("dp", "tensor")),
        P("dp", "tensor"),
        P("dp", "tensor"),
        P("dp", "tensor"),
        P("dp", "tensor"),
        P(),
    )
    return jax.shard_map(
        local,
        mesh=mesh,
        in_specs=placed,
        out_specs=(
            P(None, ("dp", "tensor")),
            P(None, ("dp", "tensor")),
            P(None, "dp", "tensor"),
            P(None, "dp", "tensor"),
            P("dp"),
            P(("dp", "tensor")),
            P(("dp", "tensor")),
            P(("dp", "tensor")),
            P("dp", "tensor"),
            P("dp", "tensor"),
            P("dp", "tensor"),
        ),
        check_vma=False,
    )
```

profile of v0, /device:TPU:4, one launch (start us, length us, event | category | flops | bytes accessed | tf_op | source)
XLA Modules:
  0.0 515.0 jit_solution(1465619128677415151)
XLA Ops:
  10.9 4.2 add_convert_fusion.3
  16.0 7.5 %add_convert_fusion.2 = (bf16[24,49152]{1,0:T(8,128)(2,1)}, f32[24,49152]{1,0:T(8,128)}) fusion(f32[24,49152]{1,0:T(8,128)} %param.18, f32[24,49152]{1,0:T(8,128)} %param.19), kind=kLoop, calls=%fused_computation.12 | loop fusion | flops 5898240 | bytes 16515072 | tf_op jit(solution)/shard_map/convert_element_type | solution.py:20
  27.0 5.3 %fusion = bf16[56,2,12,2048]{3,1,2,0:T(2,128)(2,1)} fusion(bf16[32,2,12,768]{3,1,2,0:T(2,128)(2,1)S(1)} %bitcast.28, bf16[24,2,12,2048]{3,1,2,0:T(2,128)(2,1)S(1)} %bitcast.26), kind=kLoop, calls=%fused_computation.7 | loop fusion | flops 16515072 | bytes 9043968 | tf_op jit(solution)/shard_map/concatenate | solution.py:88
  32.3 17.6 %gather_fusion = bf16[64,2,12,2048]{3,1,2,0:T(2,128)(2,1)} fusion(bf16[56,2,12,2048]{3,1,2,0:T(2,128)(2,1)} %fusion, s32[1024]{0:T(1024)S(1)} %pad_clamp_fusion.2), kind=kCustom, calls=%fused_computation | custom fusion | bytes 12583168 | tf_op jit(solution)/shard_map/gather | solution.py:43
  49.9 9.4 %copy.29 = bf16[64,2,12,2048]{3,2,1,0:T(8,128)(2,1)} copy(bf16[64,2,12,2048]{3,1,2,0:T(2,128)(2,1)} %gather_fusion) | data formatting | bytes 12582912 | tf_op jit(solution)/shard_map/gather | solution.py:43
  59.5 7.2 %bitcast_select_fusion = bf16[128,12,2048]{2,1,0:T(8,128)(2,1)} fusion(bf16[64,2,12,2048]{3,2,1,0:T(8,128)(2,1)} %copy.29, pred[128]{0:T(512)(128)(4,1)S(1)} %broadcast_in_dim.100), kind=kLoop, calls=%fused_computation.6 | loop fusion | flops 3145728 | bytes 12583040 | tf_op jit(solution)/shard_map/jit(_where)/select_n | solution.py:43
  66.8 107.0 %all_to_all.14 = bf16[128,12,2048]{2,1,0:T(8,128)(2,1)} all-to-all(bf16[128,12,2048]{2,1,0:T(8,128)(2,1)} %bitcast_select_fusion), channel_id=1, replica_groups=mesh['dp'=64,'tensor'=2] {'dp','tensor'}, dimensions={0} | all-to-all | bytes 12582912 | tf_op jit(solution)/shard_map/all_to_all | solution.py:91
  173.8 10.7 %all_to_all.10 = bf16[1536,2048]{1,0:T(8,128)(2,1)} reshape(bf16[128,12,2048]{2,1,0:T(8,128)(2,1)} %all_to_all.14) | data formatting | bytes 12582912 | tf_op jit(solution)/shard_map/all_to_all | solution.py:91
  184.5 16.2 %fusion.8 = f32[1536,1536]{1,0:T(8,128)} fusion(bf16[1536,2048]{1,0:T(8,128)(2,1)} %all_to_all.10), kind=kOutput, calls=%fused_computation.48 | convolution fusion | flops 9663676416 | bytes 15728640 | tf_op jit(solution)/shard_map/rc,sc->rs/dot_general | solution.py:99
  200.8 18.6 %reduce-scatter.3.cloned.1.call-done = f32[768,1536]{1,0:T(8,128)} async-done(((f32[1536,1536]{1,0:T(8,128)}), f32[768,1536]{1,0:T(8,128)}) %reduce-scatter.3.cloned.1.call-update) | async-done | bytes 4718608 | tf_op jit(solution)/shard_map/reduce_scatter | solution.py:98
  227.3 4.3 divide_convert_fusion.1
  231.7 18.6 %all-gather.5.cloned.1.call-done = bf16[1536,1536]{1,0:T(8,128)(2,1)} async-done(((bf16[768,1536]{1,0:T(8,128)(2,1)}), bf16[1536,1536]{1,0:T(8,128)(2,1)}) %all-gather.5.cloned.1.call-update) | async-done | bytes 4718608 | tf_op jit(solution)/shard_map/all_gather | solution.py:113
  250.3 9.1 %add_convert_fusion.1 = bf16[768,1536]{1,0:T(8,128)(2,1)} fusion(bf16[768,1536]{1,0:T(8,128)(2,1)} %divide_convert_fusion.1, bf16[1536,1536]{1,0:T(8,128)(2,1)} %all-gather.5.cloned.1.call-done), kind=kOutput, calls=%fused_computation.9 | convolution fusion | flops 3629776896 | bytes 9437184 | tf_op jit(solution)/shard_map/dot_general | solution.py:111
  259.7 18.4 %all-gather.7.cloned.1.call-done = bf16[1536,1536]{1,0:T(8,128)(2,1)} async-done(((bf16[768,1536]{1,0:T(8,128)(2,1)}), bf16[1536,1536]{1,0:T(8,128)(2,1)}) %all-gather.7.cloned.1.call-update) | async-done | bytes 4718608 | tf_op jit(solution)/shard_map/all_gather | solution.py:120
  278.1 14.9 %divide_convert_fusion = bf16[1536,2048]{1,0:T(8,128)(2,1)S(1)} fusion(bf16[1536,2048]{1,0:T(8,128)(2,1)} %all_to_all.10, bf16[1536,1536]{1,0:T(8,128)(2,1)} %all-gather.7.cloned.1.call-done, f32[]{:T(128)S(6)} %sqrt.13), kind=kOutput, calls=%fused_computation.5 | convolution fusion | flops 9679405056 | bytes 17301508 | tf_op jit(solution)/shard_map/dot_general | solution.py:119
  295.6 12.7 %fusion.9 = f32[1536,1536]{1,0:T(8,128)} fusion(bf16[1536,2048]{1,0:T(8,128)(2,1)S(1)} %divide_convert_fusion), kind=kOutput, calls=%fused_computation.49 | convolution fusion | flops 9663676416 | bytes 15728640 | tf_op jit(solution)/shard_map/rc,sc->rs/dot_general | solution.py:99
  308.4 22.0 %reduce-scatter.5.cloned.1.call-done = f32[768,1536]{1,0:T(8,128)} async-done(((f32[1536,1536]{1,0:T(8,128)}), f32[768,1536]{1,0:T(8,128)}) %reduce-scatter.5.cloned.1.call-update) | async-done | bytes 4718608 | tf_op jit(solution)/shard_map/reduce_scatter | solution.py:98
  334.7 18.5 %all-gather.9.cloned.1.call-done = bf16[1536,1536]{1,0:T(8,128)(2,1)} async-done(((bf16[768,1536]{1,0:T(8,128)(2,1)}), bf16[1536,1536]{1,0:T(8,128)(2,1)}) %all-gather.9.cloned.1.call-update) | async-done | bytes 4718608 | tf_op jit(solution)/shard_map/all_gather | solution.py:113
  353.2 9.1 %add_convert_fusion = bf16[768,1536]{1,0:T(8,128)(2,1)} fusion(bf16[768,1536]{1,0:T(8,128)(2,1)} %convert_element_type.49, bf16[1536,1536]{1,0:T(8,128)(2,1)} %all-gather.9.cloned.1.call-done), kind=kOutput, calls=%fused_computation.8 | convolution fusion | flops 3629776896 | bytes 9437184 | tf_op jit(solution)/shard_map/dot_general | solution.py:111
  363.6 17.4 %all-gather.11.cloned.1.call-done = bf16[1536,1536]{1,0:T(8,128)(2,1)} async-done(((bf16[768,1536]{1,0:T(8,128)(2,1)}), bf16[1536,1536]{1,0:T(8,128)(2,1)}) %all-gather.11.cloned.1.call-update) | async-done | bytes 4718608 | tf_op jit(solution)/shard_map/all_gather | solution.py:120
  380.9 16.6 %multiply_convert_fusion = bf16[1536,2048]{1,0:T(8,128)(2,1)} fusion(bf16[1536,2048]{1,0:T(8,128)(2,1)} %copy-done.13, bf16[1536,1536]{1,0:T(8,128)(2,1)} %all-gather.11.cloned.1.call-done, f32[]{:T(128)S(6)} %select_n.54), kind=kOutput, calls=%fused_computation.4 | convolution fusion | flops 9679405056 | bytes 17301508 | tf_op jit(solution)/shard_map/dot_general | solution.py:119
  397.6 10.7 %all-to-all-start.1 = ((bf16[64,24,2048]{2,1,0:T(8,128)(2,1)}), bf16[64,24,2048]{2,1,0:T(8,128)(2,1)}, u32[]{:S(2)}, u32[]{:S(2)}) async-start(bf16[64,24,2048]{2,1,0:T(8,128)(2,1)} %bitcast.27), calls=%async_computation.3 | async-start | bytes 12582912 | tf_op jit(solution)/shard_map/all_to_all | solution.py:129
  412.6 84.5 %all-to-all-done.1 = bf16[64,24,2048]{2,1,0:T(8,128)(2,1)} async-done(((bf16[64,24,2048]{2,1,0:T(8,128)(2,1)}), bf16[64,24,2048]{2,1,0:T(8,128)(2,1)}, u32[]{:S(2)}, u32[]{:S(2)}) %all-to-all-start.1) | async-done | bytes 6291488 | tf_op jit(solution)/shard_map/all_to_all | solution.py:129
  501.8 5.0 gather_fusion.2
  (68 shorter events, 31.1 us)
Async XLA Ops:
  7.2 212.2 %reduce-scatter.3.cloned.1.call-start = ((), (), s32[]{:S(2)}) async-start(), calls=%async_computation.4 | async-start | bytes 14155776 | tf_op jit(solution)/shard_map/reduce_scatter | solution.py:98
  9.4 1.0 copy-start.9
  10.3 0.5 copy-start.11
  200.7 49.6 %all-gather.5.cloned.1.call-start = ((), (), s32[]{:S(2)}) async-start(), calls=%async_computation.5 | async-start | bytes 7077888 | tf_op jit(solution)/shard_map/all_gather | solution.py:113
  231.6 46.4 %all-gather.7.cloned.1.call-start = ((), (), s32[]{:S(2)}) async-start(), calls=%async_computation.6 | async-start | bytes 7077888 | tf_op jit(solution)/shard_map/all_gather | solution.py:120
  259.4 71.0 %reduce-scatter.5.cloned.1.call-start = ((), (), s32[]{:S(2)}) async-start(), calls=%async_computation.7 | async-start | bytes 14155776 | tf_op jit(solution)/shard_map/reduce_scatter | solution.py:98
  293.0 2.7 copy-start.13
  308.4 44.8 %all-gather.9.cloned.1.call-start = ((), (), s32[]{:S(2)}) async-start(), calls=%async_computation.8 | async-start | bytes 7077888 | tf_op jit(solution)/shard_map/all_gather | solution.py:113
  334.5 27.8 %copy-start.12 = (s32[32]{0:T(128)S(1)}, s32[32]{0:T(128)}, u32[]{:S(2)}) copy-start(s32[32]{0:T(128)} %copy-done.11) | copy-start | bytes 388
  334.5 46.5 %all-gather.11.cloned.1.call-start = ((), (), s32[]{:S(2)}) async-start(), calls=%async_computation.9 | async-start | bytes 7077888 | tf_op jit(solution)/shard_map/all_gather | solution.py:120
  397.5 10.8 %copy-start.10 = (s32[24]{0:T(128)S(1)}, s32[24]{0:T(128)}, u32[]{:S(2)}) copy-start(s32[24]{0:T(128)} %copy-done.9) | copy-start | bytes 292
  397.6 12.8 %copy-start.8 = (s32[16,2]{0,1:T(2,128)S(1)}, s32[16,2]{0,1:T(2,128)}, u32[]{:S(2)}) copy-start(s32[16,2]{0,1:T(2,128)} %param.31) | copy-start | bytes 388
  397.6 12.9 %copy-start.4 = (f32[1344]{0:T(1024)S(1)}, f32[1344]{0:T(1024)}, u32[]{:S(2)}) copy-start(f32[1344]{0:T(1024)} %param.23) | copy-start | bytes 16132
  397.6 12.9 %copy-start.5 = (f32[1344]{0:T(1024)S(1)}, f32[1344]{0:T(1024)}, u32[]{:S(2)}) copy-start(f32[1344]{0:T(1024)} %param.24) | copy-start | bytes 16132
  397.6 12.9 %copy-start.6 = (f32[1344]{0:T(1024)S(1)}, f32[1344]{0:T(1024)}, u32[]{:S(2)}) copy-start(f32[1344]{0:T(1024)} %param.25) | copy-start | bytes 16132
  397.6 12.9 %copy-start.7 = (f32[1344]{0:T(1024)S(1)}, f32[1344]{0:T(1024)}, u32[]{:S(2)}) copy-start(f32[1344]{0:T(1024)} %param.26) | copy-start | bytes 16132
  397.6 13.5 %copy-start = (f32[128,768]{1,0:T(8,128)S(1)}, f32[128,768]{1,0:T(8,128)}, u32[]{:S(2)}) copy-start(f32[128,768]{1,0:T(8,128)} %param.30) | copy-start | bytes 1179652
  397.6 13.5 %copy-start.1 = (f32[128,768]{1,0:T(8,128)S(1)}, f32[128,768]{1,0:T(8,128)}, u32[]{:S(2)}) copy-start(f32[128,768]{1,0:T(8,128)} %param.28) | copy-start | bytes 1179652
  397.6 13.5 %copy-start.2 = (f32[128,768]{1,0:T(8,128)S(1)}, f32[128,768]{1,0:T(8,128)}, u32[]{:S(2)}) copy-start(f32[128,768]{1,0:T(8,128)} %param.27) | copy-start | bytes 1179652
  397.6 13.5 %copy-start.3 = (f32[128,768]{1,0:T(8,128)S(1)}, f32[128,768]{1,0:T(8,128)}, u32[]{:S(2)}) copy-start(f32[128,768]{1,0:T(8,128)} %param.29) | copy-start | bytes 1179652
  397.6 99.5 %all-to-all-start.1 = ((bf16[64,24,2048]{2,1,0:T(8,128)(2,1)}), bf16[64,24,2048]{2,1,0:T(8,128)(2,1)}, u32[]{:S(2)}, u32[]{:S(2)}) async-start(bf16[64,24,2048]{2,1,0:T(8,128)(2,1)} %bitcast.27), calls=%async_computation.3 | async-start | bytes 12582912 | tf_op jit(solution)/shard_map/all_to_all | solution.py:129
Sparse Core Ops, SparseCore 0:
  200.8 18.4 reduce-scatter.2
  231.8 18.5 all-gather.4
  259.5 18.4 all-gather.6
  308.5 21.8 reduce-scatter.4
  334.6 18.5 all-gather.8
  362.4 18.4 all-gather.10
where the time goes:
time: 524 us; the launch traced here: 515 us
  waiting for transfers between devices  198 us (38%)
  blocking collectives  110 us (21%)
  matrix products  78.6 us (15%)
  local copies, waits for them, and re-layouts  55 us (10%)
  other arithmetic  43.4 us (8%)
  between operations  18.5 us (4%)
  starting transfers between devices  11.3 us (2%)
    all_to_all x1, blocking collectives, local(): lax.all_to_all(outgoing.reshape(D, slot_width), ('dp', 'tensor'), split_a...  107 us
    all_to_all x1, waiting for transfers between devices, local(): lax.all_to_all(iterate.reshape(wide_count, D // wide_count, slot_width),...  84.5 us
    reduce_scatter x2, waiting for transfers between devices, local(): lax.psum_scatter(jnp.einsum('rc,sc->rs', current, current, preferred_elem...  40.6 us
    all_gather x2, waiting for transfers between devices, local(): lax.all_gather(normed_part, 'tensor', axis=0, tiled=True)  37.1 us
    all_gather x2, waiting for transfers between devices, local(): lax.all_gather(polynomial, 'tensor', axis=0, tiled=True)  35.7 us
    dot_general x2, matrix products, local(): jnp.dot(lax.all_gather(polynomial, 'tensor', axis=0, tiled=True), current...  31.5 us
    dot_general x2, matrix products, local(): jnp.einsum('rc,sc->rs', current, current, preferred_element_type=jnp.floa...  29 us
    gather x2, local copies, waits for them, and re-layouts, select_pieces(): pieces[chosen]  27 us
  transfers between devices with their start and end apart: 7, of which 7 were waited for; matrix products, arithmetic and copies ran while one was open for 1% of the time, Pallas kernels for 0%

commit v1 on v0

--- a/solution.py
+++ b/solution.py
@@ -110,7 +110,15 @@
         normed_part = (gram_part / gram_scale).astype(jnp.bfloat16)
         squared = jnp.dot(
             normed_part,
-            lax.all_gather(normed_part, "tensor", axis=0, tiled=True),
+            jnp.concatenate(
+                jax.lax.all_to_all(
+                    jnp.stack([normed_part for _ in range(jax.lax.axis_size("tensor"))]),
+                    axis_name="tensor",
+                    split_axis=0,
+                    concat_axis=0,
+                ),
+                axis=0,
+            ),
             preferred_element_type=jnp.float32,
         )
         polynomial = (

time: 524 us -> 492 us (0.939)
  waiting for transfers between devices: 198 us -> 161 us
  blocking collectives: 110 us -> 126 us
  matrix products: 78.6 us -> 71.1 us
    all_gather x2 -> x0, waiting for transfers between devices: 37.1 us -> none  [local(): lax.all_gather(normed_part, 'tensor', axis=0, tiled=True)]
    all_to_all x0 -> x2, blocking collectives: none -> 15.7 us  [local(): jax.lax.all_to_all(jnp.stack([normed_part for _ in range(jax.lax.axis_siz...]
    convert_element_type x2 -> x0, other arithmetic: 8.31 us -> none  [local(): normed_part = (gram_part / gram_scale).astype(jnp.bfloat16)]
    dot_general x2, matrix products: 18.2 us -> 10.4 us  [local(): jnp.dot(normed_part, jnp.concatenate(jax.lax.all_to_all(jnp.stack([normed...]
    another operation x0 -> x4, other arithmetic: none -> 6.32 us  [local(): jnp.stack([normed_part for _ in range(jax.lax.axis_size('tensor'))])]
  transfers between devices with their start and end apart: 7 -> 5, of which waited for: 7 -> 5; matrix products, arithmetic and copies ran while one was open for 1% -> 1% of each run, Pallas kernels for 0% -> 0%
where the time goes in v1:
time: 492 us; the launch traced here: 483 us
  waiting for transfers between devices  161 us (33%)
  blocking collectives  126 us (26%)
  matrix products  71.1 us (14%)
  local copies, waits for them, and re-layouts  55 us (11%)
  other arithmetic  41.4 us (8%)
  between operations  18.2 us (4%)
  starting transfers between devices  11.3 us (2%)
    all_to_all x1, blocking collectives, local(): lax.all_to_all(outgoing.reshape(D, slot_width), ('dp', 'tensor'), split_a...  107 us
    all_to_all x1, waiting for transfers between devices, local(): lax.all_to_all(iterate.reshape(wide_count, D // wide_count, slot_width),...  84.5 us
    reduce_scatter x2, waiting for transfers between devices, local(): lax.psum_scatter(jnp.einsum('rc,sc->rs', current, current, preferred_elem...  40.6 us
    all_gather x2, waiting for transfers between devices, local(): lax.all_gather(polynomial, 'tensor', axis=0, tiled=True)  35.5 us
    dot_general x2, matrix products, local(): jnp.dot(lax.all_gather(polynomial, 'tensor', axis=0, tiled=True), current...  31.5 us
    dot_general x2, matrix products, local(): jnp.einsum('rc,sc->rs', current, current, preferred_element_type=jnp.floa...  29.2 us
    gather x2, local copies, waits for them, and re-layouts, select_pieces(): pieces[chosen]  27 us
    all_to_all x2, blocking collectives, local(): jax.lax.all_to_all(jnp.stack([normed_part for _ in range(jax.lax.axis_siz...  15.7 us
  transfers between devices with their start and end apart: 5, of which 5 were waited for; matrix products, arithmetic and copies ran while one was open for 1% of the time, Pallas kernels for 0%

profile of v1, /device:TPU:4, one launch (start us, length us, event | category | flops | bytes accessed | tf_op | source)
XLA Modules:
  0.0 483.4 jit_solution(14961899683188364699)
XLA Ops:
  10.9 4.2 add_convert_fusion.3
  16.0 7.5 %add_convert_fusion.2 = (bf16[24,49152]{1,0:T(8,128)(2,1)}, f32[24,49152]{1,0:T(8,128)}) fusion(f32[24,49152]{1,0:T(8,128)} %param.18, f32[24,49152]{1,0:T(8,128)} %param.19), kind=kLoop, calls=%fused_computation.14 | loop fusion | flops 5898240 | bytes 16515072 | tf_op jit(solution)/shard_map/convert_element_type | solution.py:20
  27.0 5.3 %fusion = bf16[56,2,12,2048]{3,1,2,0:T(2,128)(2,1)} fusion(bf16[32,2,12,768]{3,1,2,0:T(2,128)(2,1)S(1)} %bitcast.34, bf16[24,2,12,2048]{3,1,2,0:T(2,128)(2,1)S(1)} %bitcast.32), kind=kLoop, calls=%fused_computation.7 | loop fusion | flops 16515072 | bytes 9043968 | tf_op jit(solution)/shard_map/concatenate | solution.py:88
  32.3 17.6 %gather_fusion = bf16[64,2,12,2048]{3,1,2,0:T(2,128)(2,1)} fusion(bf16[56,2,12,2048]{3,1,2,0:T(2,128)(2,1)} %fusion, s32[1024]{0:T(1024)S(1)} %pad_clamp_fusion.2), kind=kCustom, calls=%fused_computation | custom fusion | bytes 12583168 | tf_op jit(solution)/shard_map/gather | solution.py:43
  49.9 9.4 %copy.29 = bf16[64,2,12,2048]{3,2,1,0:T(8,128)(2,1)} copy(bf16[64,2,12,2048]{3,1,2,0:T(2,128)(2,1)} %gather_fusion) | data formatting | bytes 12582912 | tf_op jit(solution)/shard_map/gather | solution.py:43
  59.5 7.3 %bitcast_select_fusion = bf16[128,12,2048]{2,1,0:T(8,128)(2,1)} fusion(bf16[64,2,12,2048]{3,2,1,0:T(8,128)(2,1)} %copy.29, pred[128]{0:T(512)(128)(4,1)S(1)} %broadcast_in_dim.100), kind=kLoop, calls=%fused_computation.6 | loop fusion | flops 3145728 | bytes 12583040 | tf_op jit(solution)/shard_map/jit(_where)/select_n | solution.py:43
  66.8 106.8 %all_to_all.24 = bf16[128,12,2048]{2,1,0:T(8,128)(2,1)} all-to-all(bf16[128,12,2048]{2,1,0:T(8,128)(2,1)} %bitcast_select_fusion), channel_id=1, replica_groups=mesh['dp'=64,'tensor'=2] {'dp','tensor'}, dimensions={0} | all-to-all | bytes 12582912 | tf_op jit(solution)/shard_map/all_to_all | solution.py:91
  173.6 10.7 %all_to_all.16 = bf16[1536,2048]{1,0:T(8,128)(2,1)} reshape(bf16[128,12,2048]{2,1,0:T(8,128)(2,1)} %all_to_all.24) | data formatting | bytes 12582912 | tf_op jit(solution)/shard_map/all_to_all | solution.py:91
  184.3 16.3 %fusion.10 = f32[1536,1536]{1,0:T(8,128)} fusion(bf16[1536,2048]{1,0:T(8,128)(2,1)} %all_to_all.16), kind=kOutput, calls=%fused_computation.53 | convolution fusion | flops 9663676416 | bytes 15728640 | tf_op jit(solution)/shard_map/rc,sc->rs/dot_general | solution.py:99
  200.7 18.6 %reduce-scatter.3.cloned.1.call-done = f32[768,1536]{1,0:T(8,128)} async-done(((f32[1536,1536]{1,0:T(8,128)}), f32[768,1536]{1,0:T(8,128)}) %reduce-scatter.3.cloned.1.call-update) | async-done | bytes 4718608 | tf_op jit(solution)/shard_map/reduce_scatter | solution.py:98
  219.3 4.2 multiply_reduce_fusion
  230.5 7.8 %all_to_all.25 = bf16[2,768,1536]{2,1,0:T(8,128)(2,1)S(1)} all-to-all(bf16[2,768,1536]{2,1,0:T(8,128)(2,1)S(1)} %pad_maximum_fusion), channel_id=1, replica_groups=mesh['dp'=64,'tensor'=2] {'tensor'}, dimensions={0} | all-to-all | bytes 9437184 | tf_op jit(solution)/shard_map/all_to_all | solution.py:114
  238.3 5.2 %add_convert_fusion.1 = bf16[768,1536]{1,0:T(8,128)(2,1)} fusion(bf16[1536,1536]{1,0:T(8,128)(2,1)S(1)} %bitcast.37, f32[768,1536]{1,0:T(8,128)S(1)} %bitcast.31, f32[]{:T(128)S(6)} %add.103), kind=kOutput, calls=%fused_computation.11 | convolution fusion | flops 3634495488 | bytes 11796484 | tf_op jit(solution)/shard_map/dot_general | solution.py:111
  244.1 18.1 %all-gather.3.cloned.1.call-done = bf16[1536,1536]{1,0:T(8,128)(2,1)} async-done(((bf16[768,1536]{1,0:T(8,128)(2,1)}), bf16[1536,1536]{1,0:T(8,128)(2,1)}) %all-gather.3.cloned.1.call-update) | async-done | bytes 4718608 | tf_op jit(solution)/shard_map/all_gather | solution.py:128
  262.2 14.9 %divide_convert_fusion = bf16[1536,2048]{1,0:T(8,128)(2,1)S(1)} fusion(bf16[1536,2048]{1,0:T(8,128)(2,1)} %all_to_all.16, bf16[1536,1536]{1,0:T(8,128)(2,1)} %all-gather.3.cloned.1.call-done, f32[]{:T(128)S(6)} %sqrt.13), kind=kOutput, calls=%fused_computation.5 | convolution fusion | flops 9679405056 | bytes 17301508 | tf_op jit(solution)/shard_map/dot_general | solution.py:127
  279.8 12.9 %fusion.11 = f32[1536,1536]{1,0:T(8,128)} fusion(bf16[1536,2048]{1,0:T(8,128)(2,1)S(1)} %divide_convert_fusion), kind=kOutput, calls=%fused_computation.54 | convolution fusion | flops 9663676416 | bytes 15728640 | tf_op jit(solution)/shard_map/rc,sc->rs/dot_general | solution.py:99
  292.7 22.0 %reduce-scatter.5.cloned.1.call-done = f32[768,1536]{1,0:T(8,128)} async-done(((f32[1536,1536]{1,0:T(8,128)}), f32[768,1536]{1,0:T(8,128)}) %reduce-scatter.5.cloned.1.call-update) | async-done | bytes 4718608 | tf_op jit(solution)/shard_map/reduce_scatter | solution.py:98
  317.8 7.9 %all_to_all.26 = bf16[2,768,1536]{2,1,0:T(8,128)(2,1)S(1)} all-to-all(bf16[2,768,1536]{2,1,0:T(8,128)(2,1)S(1)} %pad_maximum_fusion.1), channel_id=1, replica_groups=mesh['dp'=64,'tensor'=2] {'tensor'}, dimensions={0} | all-to-all | bytes 9437184 | tf_op jit(solution)/shard_map/all_to_all | solution.py:114
  325.7 5.2 %add_convert_fusion = bf16[768,1536]{1,0:T(8,128)(2,1)} fusion(bf16[1536,1536]{1,0:T(8,128)(2,1)S(1)} %bitcast.38, f32[768,1536]{1,0:T(8,128)S(1)} %bitcast.36), kind=kOutput, calls=%fused_computation.10 | convolution fusion | flops 3632136192 | bytes 11796480 | tf_op jit(solution)/shard_map/dot_general | solution.py:111
  332.3 17.4 %all-gather.5.cloned.1.call-done = bf16[1536,1536]{1,0:T(8,128)(2,1)} async-done(((bf16[768,1536]{1,0:T(8,128)(2,1)}), bf16[1536,1536]{1,0:T(8,128)(2,1)}) %all-gather.5.cloned.1.call-update) | async-done | bytes 4718608 | tf_op jit(solution)/shard_map/all_gather | solution.py:128
  349.7 16.6 %multiply_convert_fusion = bf16[1536,2048]{1,0:T(8,128)(2,1)} fusion(bf16[1536,2048]{1,0:T(8,128)(2,1)} %copy-done.13, bf16[1536,1536]{1,0:T(8,128)(2,1)} %all-gather.5.cloned.1.call-done, f32[]{:T(128)S(6)} %select_n.54), kind=kOutput, calls=%fused_computation.4 | convolution fusion | flops 9679405056 | bytes 17301508 | tf_op jit(solution)/shard_map/dot_general | solution.py:127
  366.4 10.7 %all-to-all-start.3 = ((bf16[64,24,2048]{2,1,0:T(8,128)(2,1)}), bf16[64,24,2048]{2,1,0:T(8,128)(2,1)}, u32[]{:S(2)}, u32[]{:S(2)}) async-start(bf16[64,24,2048]{2,1,0:T(8,128)(2,1)} %bitcast.33), calls=%async_computation.5 | async-start | bytes 12582912 | tf_op jit(solution)/shard_map/all_to_all | solution.py:137
  381.4 84.5 %all-to-all-done.3 = bf16[64,24,2048]{2,1,0:T(8,128)(2,1)} async-done(((bf16[64,24,2048]{2,1,0:T(8,128)(2,1)}), bf16[64,24,2048]{2,1,0:T(8,128)(2,1)}, u32[]{:S(2)}, u32[]{:S(2)}) %all-to-all-start.3) | async-done | bytes 6291488 | tf_op jit(solution)/shard_map/all_to_all | solution.py:137
  470.6 5.0 %gather_fusion.2 = bf16[24,24,2048]{2,1,0:T(8,128)(2,1)} fusion(bf16[64,24,2048]{2,1,0:T(8,128)(2,1)} %all-to-all-done.3, s32[1024]{0:T(1024)S(1)} %pad_clamp_fusion), kind=kCustom, calls=%fused_computation.2 | custom fusion | bytes 4718688 | tf_op jit(solution)/shard_map/gather | solution.py:145
  (76 shorter events, 29.2 us)
Async XLA Ops:
  7.2 212.1 %reduce-scatter.3.cloned.1.call-start = ((), (), s32[]{:S(2)}) async-start(), calls=%async_computation.6 | async-start | bytes 14155776 | tf_op jit(solution)/shard_map/reduce_scatter | solution.py:98
  9.4 1.0 copy-start.9
  10.3 0.5 copy-start.11
  200.6 61.6 %all-gather.3.cloned.1.call-start = ((), (), s32[]{:S(2)}) async-start(), calls=%async_computation.7 | async-start | bytes 7077888 | tf_op jit(solution)/shard_map/all_gather | solution.py:128
  230.1 8.2 %slice-start = ((s8[4718592]{0:T(1024)(128)(4,1)}), s8[524288]{0:T(1024)(128)(4,1)S(1)}, s32[]{:S(2)}) async-start(s8[4718592]{0:T(1024)(128)(4,1)} %bitcast.30), calls=%async_computation.10 | async-start | bytes 1048576
  230.5 7.8 %slice-start.1 = ((s8[4718592]{0:T(1024)(128)(4,1)}), s8[4194304]{0:T(1024)(128)(4,1)S(1)}, s32[]{:S(2)}) async-start(s8[4718592]{0:T(1024)(128)(4,1)} %bitcast.30), calls=%async_computation.11 | async-start | bytes 8388608
  243.5 71.2 %reduce-scatter.5.cloned.1.call-start = ((), (), s32[]{:S(2)}) async-start(), calls=%async_computation.8 | async-start | bytes 14155776 | tf_op jit(solution)/shard_map/reduce_scatter | solution.py:98
  277.1 2.7 copy-start.13
  292.7 57.0 %all-gather.5.cloned.1.call-start = ((), (), s32[]{:S(2)}) async-start(), calls=%async_computation.9 | async-start | bytes 7077888 | tf_op jit(solution)/shard_map/all_gather | solution.py:128
  317.3 8.4 %slice-start.2 = ((s8[4718592]{0:T(1024)(128)(4,1)}), s8[524288]{0:T(1024)(128)(4,1)S(1)}, s32[]{:S(2)}) async-start(s8[4718592]{0:T(1024)(128)(4,1)} %bitcast.35), calls=%async_computation.12 | async-start | bytes 1048576
  317.7 8.0 %slice-start.3 = ((s8[4718592]{0:T(1024)(128)(4,1)}), s8[4194304]{0:T(1024)(128)(4,1)S(1)}, s32[]{:S(2)}) async-start(s8[4718592]{0:T(1024)(128)(4,1)} %bitcast.35), calls=%async_computation.13 | async-start | bytes 8388608
  325.7 5.3 %copy-start.12 = (s32[32]{0:T(128)S(1)}, s32[32]{0:T(128)}, u32[]{:S(2)}) copy-start(s32[32]{0:T(128)} %copy-done.11) | copy-start | bytes 388
  366.3 10.8 %copy-start.10 = (s32[24]{0:T(128)S(1)}, s32[24]{0:T(128)}, u32[]{:S(2)}) copy-start(s32[24]{0:T(128)} %copy-done.9) | copy-start | bytes 292
  366.3 12.8 %copy-start.8 = (s32[16,2]{0,1:T(2,128)S(1)}, s32[16,2]{0,1:T(2,128)}, u32[]{:S(2)}) copy-start(s32[16,2]{0,1:T(2,128)} %param.31) | copy-start | bytes 388
  366.3 12.9 %copy-start.4 = (f32[1344]{0:T(1024)S(1)}, f32[1344]{0:T(1024)}, u32[]{:S(2)}) copy-start(f32[1344]{0:T(1024)} %param.23) | copy-start | bytes 16132
  366.3 12.9 %copy-start.5 = (f32[1344]{0:T(1024)S(1)}, f32[1344]{0:T(1024)}, u32[]{:S(2)}) copy-start(f32[1344]{0:T(1024)} %param.24) | copy-start | bytes 16132
  366.3 12.9 %copy-start.6 = (f32[1344]{0:T(1024)S(1)}, f32[1344]{0:T(1024)}, u32[]{:S(2)}) copy-start(f32[1344]{0:T(1024)} %param.25) | copy-start | bytes 16132
  366.3 12.9 %copy-start.7 = (f32[1344]{0:T(1024)S(1)}, f32[1344]{0:T(1024)}, u32[]{:S(2)}) copy-start(f32[1344]{0:T(1024)} %param.26) | copy-start | bytes 16132
  366.3 13.5 %copy-start = (f32[128,768]{1,0:T(8,128)S(1)}, f32[128,768]{1,0:T(8,128)}, u32[]{:S(2)}) copy-start(f32[128,768]{1,0:T(8,128)} %param.30) | copy-start | bytes 1179652
  366.4 13.5 %copy-start.1 = (f32[128,768]{1,0:T(8,128)S(1)}, f32[128,768]{1,0:T(8,128)}, u32[]{:S(2)}) copy-start(f32[128,768]{1,0:T(8,128)} %param.28) | copy-start | bytes 1179652
  366.4 13.5 %copy-start.2 = (f32[128,768]{1,0:T(8,128)S(1)}, f32[128,768]{1,0:T(8,128)}, u32[]{:S(2)}) copy-start(f32[128,768]{1,0:T(8,128)} %param.27) | copy-start | bytes 1179652
  366.4 13.5 %copy-start.3 = (f32[128,768]{1,0:T(8,128)S(1)}, f32[128,768]{1,0:T(8,128)}, u32[]{:S(2)}) copy-start(f32[128,768]{1,0:T(8,128)} %param.29) | copy-start | bytes 1179652
  366.4 99.5 %all-to-all-start.3 = ((bf16[64,24,2048]{2,1,0:T(8,128)(2,1)}), bf16[64,24,2048]{2,1,0:T(8,128)(2,1)}, u32[]{:S(2)}, u32[]{:S(2)}) async-start(bf16[64,24,2048]{2,1,0:T(8,128)(2,1)} %bitcast.33), calls=%async_computation.5 | async-start | bytes 12582912 | tf_op jit(solution)/shard_map/all_to_all | solution.py:137
Sparse Core Ops, SparseCore 0:
  200.7 18.4 reduce-scatter.2
  243.7 18.5 all-gather.2
  292.8 21.8 reduce-scatter.4
  331.1 18.5 all-gather.4
